TPU v7x, 32 devices: a whole 2x2x4 slice. The times are simulated.
32 devices in a mesh: tm: 4 (over y, core), space: 8 (over z, x).
Axes of the slice: x: 2, y: 2, z: 4, core: 2. Of those that a mesh axis runs over, the one named last changes fastest.
Arguments:
- first_state: float32 [16, 64, 256], P(None, 'space'), may hold values from -6 to 6
- time_embed: float32 [4, 320], P('tm'), may hold values from -6 to 6
- drift_scale: float32 [4], P('tm'), may hold values from 0.05 to 0.25
- state_decay: float32 [4], P('tm'), may hold values from 0.01 to 0.1
- lift_weight: bfloat16 [320, 16], replicated, may hold values from -1.5 to 1.5
- conv_one: bfloat16 [3, 3, 320, 320], replicated, may hold values from -0.109375 to 0.109375
- conv_two: bfloat16 [3, 3, 320, 320], replicated, may hold values from -0.109375 to 0.109375
- project_weight: bfloat16 [16, 320], replicated, may hold values from -0.3125 to 0.3125
Outputs:
- trajectory: float32 [4, 16, 64, 256], P('tm', None, 'space')
All inputs are finite; a program needn't handle non-finite values.
Results may differ from a plain program's by a relative error of at most 0.0019.
Values may be sent and summed in bfloat16 or wider, within the bound.
A program may use at most 128 MiB of HBM per device.

v0:
```python
import jax
import jax.numpy as jnp
from jax import lax
from jax.sharding import PartitionSpec as P

ITERS = 2


def with_halo(block, sides, width):
    for axis, dim in sides:
        count = lax.axis_size(axis)
        forward = [(i, i + 1) for i in range(count - 1)]
        backward = [(target, source) for source, target in forward]
        low = lax.ppermute(
            lax.slice_in_dim(block, block.shape[dim] - width, None, axis=dim), axis, forward
        )
        high = lax.ppermute(lax.slice_in_dim(block, 0, width, axis=dim), axis, backward)
        block = jnp.concatenate([low, block, high], axis=dim)
    return block


def prefix(value, axis, join, neutral):
    count, mine = (lax.axis_size(axis), lax.axis_index(axis))
    pieces = lax.all_gather(value, axis)
    subtotal = jnp.full_like(value, 0) + jnp.asarray(neutral, value.dtype)

    def turn(position, subtotal):
        longer = join(subtotal, pieces[position])
        return jnp.where(position < mine, longer, subtotal)

    return lax.fori_loop(0, count - 1, turn, subtotal)


def shift_columns(field, col_tap):
    spread = [(0, 0)] * (field.ndim - 1)
    if col_tap == 0:
        return jnp.pad(field[..., :-1], spread + [(1, 0)])
    if col_tap == 2:
        return jnp.pad(field[..., 1:], spread + [(0, 1)])
    return field


def convolve(active, weight):
    out_rows = active.shape[2] - 2
    total = None
    for row_tap in range(3):
        rows_view = active[:, :, row_tap : row_tap + out_rows]
        for col_tap in range(3):
            term = jnp.einsum(
                "oi,tirw->torw",
                weight[row_tap, col_tap],
                shift_columns(rows_view, col_tap),
                preferred_element_type=jnp.float32,
            )
            total = term if total is None else total + term
    return total


def add_pair(earlier, later):
    return earlier + later


def denoise(states, time_embed, lift_weight, conv_one, conv_two, project_weight):
    embed = time_embed[:, :, None, None]
    lifted = (
        jnp.einsum(
            "fc,tcrw->tfrw",
            lift_weight,
            states.astype(jnp.bfloat16),
            preferred_element_type=jnp.float32,
        )
        + embed
    )
    active = with_halo(jax.nn.silu(lifted).astype(jnp.bfloat16), (("space", 2),), 1)
    first = lifted + convolve(active, conv_one)
    active = with_halo(jax.nn.silu(first).astype(jnp.bfloat16), (("space", 2),), 1)
    second = first + convolve(active, conv_two)
    active = jax.nn.silu(second).astype(jnp.bfloat16)
    return jnp.einsum("cf,tfrw->tcrw", project_weight, active, preferred_element_type=jnp.float32)


def per_device(
    first_state,
    time_embed,
    drift_scale,
    state_decay,
    lift_weight,
    conv_one,
    conv_two,
    project_weight,
):
    states = first_state[None]
    running = jnp.zeros_like(states)
    earlier_sum = jnp.zeros_like(first_state)
    for sweep in range(ITERS):
        outputs = denoise(states, time_embed, lift_weight, conv_one, conv_two, project_weight)
        drifts = (
            drift_scale[:, None, None, None] * outputs - state_decay[:, None, None, None] * states
        )
        running = jnp.cumsum(drifts, axis=0)
        block_total = running[-1]
        earlier_sum = prefix(block_total, "tm", add_pair, jnp.zeros_like(block_total))
        if sweep + 1 < ITERS:
            shifted = jnp.concatenate([jnp.zeros_like(running), running[:-1]], axis=0)
            states = first_state[None] + (earlier_sum[None] + shifted)
    return first_state[None] + (earlier_sum[None] + running)


def solution(mesh):
    in_specs = (P(None, "space", None), P("tm", None), P("tm"), P("tm"), P(), P(), P(), P())
    out_specs = P("tm", None, "space", None)
    return jax.shard_map(
        per_device, mesh=mesh, in_specs=in_specs, out_specs=out_specs, check_vma=False
    )
```

profile of v0, /device:TPU:0, one launch (start us, length us, event | category | flops | bytes accessed | tf_op | source)
XLA Modules:
  0.0 161.4 jit_solution(16445888927007760506)
XLA Ops:
  4.0 4.9 %collective-permute-start = (bf16[1,320,1,256]{3,1,2,0:T(8,128)(2,1)S(1)}, bf16[1,320,1,256]{3,1,2,0:T(8,128)(2,1)S(1)}, u32[]{:S(2)}, u32[]{:S(2)}) collective-permute-start(bf16[1,320,1,256]{3,1,2,0:T(8,128)(2,1)S(1)} %get-tuple-element.241), channel_id=1, source_target_pairs={{0,1},{1,2},{2,3},{3,4},{4,5},{5,6},{6,7},{8,9},{9,10},{10,11},{11... | collective-permute-start | bytes 491528 | tf_op jit(solution)/shard_map/ppermute | solution.py:14
  10.2 3.3 %fusion.160 = f32[8,256,320]{1,2,0:T(8,128)} fusion(bf16[1,320,8,256]{3,1,2,0:T(8,128)(2,1)S(1)} %get-tuple-element.243, bf16[3,3,320,320]{3,2,1,0:T(8,128)(2,1)} %param.17), kind=kOutput, calls=%fused_computation.185 | convolution fusion | flops 419430400 | bytes 4177920 | tf_op jit(solution)/shard_map/oi,tirw->torw/dot_general | solution.py:49
  23.3 2.4 %fusion.68 = f32[8,256,320]{1,2,0:T(8,128)} fusion(bf16[1,320,8,256]{3,1,2,0:T(8,128)(2,1)S(1)} %get-tuple-element.243, bf16[1,320,1,256]{3,1,2,0:T(8,128)(2,1)S(1)} %collective-permute-done, bf16[3,3,320,320]{3,2,1,0:T(8,128)(2,1)S(1)} %copy-done.3), kind=kOutput, calls=%fused_computation.109 | convolution fusion | flops 424017920 | bytes 4341760 | tf_op jit(solution)/shard_map/oi,tirw->torw/dot_general | solution.py:49
  28.1 6.1 %multiply_convert_fusion.3 = (bf16[1,320,8,256]{3,1,2,0:T(8,128)(2,1)S(1)}, f32[1,320,8,256]{3,1,2,0:T(8,128)}) fusion(bf16[1,320,1,256]{3,1,2,0:T(8,128)(2,1)S(1)} %collective-permute-done.1, bf16[1,320,8,256]{3,1,2,0:T(8,128)(2,1)S(1)} %get-tuple-element.243, bf16[3,3,320,320]{3,2,1,0:T(8,128)(2,1)S(1)} %copy-done.3, f32[8,256,320]{1,2,0:T(8,128)} %fusion.58, ...), kind=kOutput, calls=%fused_computation.38 | convolution fusion | flops 433848320 | bytes 29247488 | tf_op jit(solution)/shard_map/oi,tirw->torw/dot_general | solution.py:49
  34.3 4.4 %collective-permute-start.2 = (bf16[1,320,1,256]{3,1,2,0:T(8,128)(2,1)S(1)}, bf16[1,320,1,256]{3,1,2,0:T(8,128)(2,1)S(1)}, u32[]{:S(2)}, u32[]{:S(2)}) collective-permute-start(bf16[1,320,1,256]{3,1,2,0:T(8,128)(2,1)S(1)} %get-tuple-element.235), channel_id=1, source_target_pairs={{0,1},{1,2},{2,3},{3,4},{4,5},{5,6},{6,7},{8,9},{9,10},{10,11},{11... | collective-permute-start | bytes 491528 | tf_op jit(solution)/shard_map/ppermute | solution.py:14
  42.6 3.9 %collective-permute-done.3 = bf16[1,320,1,256]{3,1,2,0:T(8,128)(2,1)S(1)} collective-permute-done((bf16[1,320,1,256]{3,1,2,0:T(8,128)(2,1)S(1)}, bf16[1,320,1,256]{3,1,2,0:T(8,128)(2,1)S(1)}, u32[]{:S(2)}, u32[]{:S(2)}) %collective-permute-start.3) | collective-permute-done | bytes 163872 | tf_op jit(solution)/shard_map/ppermute | solution.py:17
  47.2 2.5 %fusion.146 = f32[8,256,320]{1,2,0:T(8,128)} fusion(bf16[1,320,8,255]{3,1,2,0:T(8,128)(2,1)S(1)} %get-tuple-element.232, bf16[3,3,320,320]{3,2,1,0:T(8,128)(2,1)S(1)} %copy-done.5), kind=kOutput, calls=%fused_computation.171 | convolution fusion | flops 419430400 | bytes 4177920 | tf_op jit(solution)/shard_map/oi,tirw->torw/dot_general | solution.py:49
  52.0 2.5 %fusion.152 = f32[8,256,320]{1,2,0:T(8,128)} fusion(bf16[1,320,8,255]{3,1,2,0:T(8,128)(2,1)S(1)} %get-tuple-element.234, bf16[3,3,320,320]{3,2,1,0:T(8,128)(2,1)S(1)} %copy-done.5), kind=kOutput, calls=%fused_computation.177 | convolution fusion | flops 419430400 | bytes 4177920 | tf_op jit(solution)/shard_map/oi,tirw->torw/dot_general | solution.py:49
  54.6 2.5 %fusion.154 = f32[8,256,320]{1,2,0:T(8,128)} fusion(bf16[1,320,8,255]{3,1,2,0:T(8,128)(2,1)S(1)} %get-tuple-element.231, bf16[3,3,320,320]{3,2,1,0:T(8,128)(2,1)S(1)} %copy-done.5), kind=kOutput, calls=%fused_computation.179 | convolution fusion | flops 419430400 | bytes 4177920 | tf_op jit(solution)/shard_map/oi,tirw->torw/dot_general | solution.py:49
  59.3 2.4 %fusion.77 = f32[8,256,320]{1,2,0:T(8,128)} fusion(bf16[1,320,8,256]{3,1,2,0:T(8,128)(2,1)S(1)} %get-tuple-element.245, bf16[1,320,1,256]{3,1,2,0:T(8,128)(2,1)S(1)} %collective-permute-done.2, bf16[3,3,320,320]{3,2,1,0:T(8,128)(2,1)S(1)} %copy-done.5), kind=kOutput, calls=%fused_computation.114 | convolution fusion | flops 424017920 | bytes 4341760 | tf_op jit(solution)/shard_map/oi,tirw->torw/dot_general | solution.py:49
  64.2 10.0 %fusion.194 = f32[1,16,8,256]{3,1,2,0:T(8,128)S(1)} fusion(f32[1,320,8,256]{3,1,2,0:T(8,128)} %get-tuple-element.246, f32[8,256,320]{1,2,0:T(8,128)} %fusion.48, f32[8,256,320]{1,2,0:T(8,128)} %fusion.146, f32[8,256,320]{1,2,0:T(8,128)} %fusion.148, f32[8,256,320]{1,2,0:T(8,128)} %fusion.150, f32[8,256,320]{1,2,0:T(8,128)} %fusion.152, ...), kind=kOutput, calls=%fused_computation.211 | convolution fusion | flops 454262784 | bytes 25586688 | tf_op jit(solution)/shard_map/cf,tfrw->tcrw/dot_general | solution.py:79
  74.2 7.2 %all_gather.6 = f32[4,16,8,256]{3,2,1,0:T(8,128)S(1)} all-gather(f32[1,16,8,256]{3,2,1,0:T(8,128)S(1)} %copy.21), channel_id=1, replica_groups=mesh['tm'=4,'space'=8] {'tm'}, dimensions={0}, use_global_device_ids=true | all-gather | bytes 655360 | tf_op jit(solution)/shard_map/all_gather | solution.py:24
  82.6 4.5 %collective-permute-start.4 = (bf16[1,320,1,256]{3,1,2,0:T(8,128)(2,1)S(1)}, bf16[1,320,1,256]{3,1,2,0:T(8,128)(2,1)S(1)}, u32[]{:S(2)}, u32[]{:S(2)}) collective-permute-start(bf16[1,320,1,256]{3,1,2,0:T(8,128)(2,1)S(1)} %get-tuple-element.229), channel_id=1, source_target_pairs={{0,1},{1,2},{2,3},{3,4},{4,5},{5,6},{6,7},{8,9},{9,10},{10,11},{11... | collective-permute-start | bytes 491528 | tf_op jit(solution)/shard_map/ppermute | solution.py:14
  91.1 4.3 %collective-permute-done.5 = bf16[1,320,1,256]{3,1,2,0:T(8,128)(2,1)S(1)} collective-permute-done((bf16[1,320,1,256]{3,1,2,0:T(8,128)(2,1)S(1)}, bf16[1,320,1,256]{3,1,2,0:T(8,128)(2,1)S(1)}, u32[]{:S(2)}, u32[]{:S(2)}) %collective-permute-start.5) | collective-permute-done | bytes 163872 | tf_op jit(solution)/shard_map/ppermute | solution.py:17
  102.2 2.5 %fusion.86 = f32[8,256,320]{1,2,0:T(8,128)} fusion(bf16[1,320,8,256]{3,1,2,0:T(8,128)(2,1)S(1)} %get-tuple-element.247, bf16[1,320,1,256]{3,1,2,0:T(8,128)(2,1)S(1)} %collective-permute-done.4, bf16[3,3,320,320]{3,2,1,0:T(8,128)(2,1)S(1)} %copy-done.4), kind=kOutput, calls=%fused_computation.119 | convolution fusion | flops 424017920 | bytes 4341760 | tf_op jit(solution)/shard_map/oi,tirw->torw/dot_general | solution.py:49
  107.1 6.1 %multiply_convert_fusion.1 = (bf16[1,320,8,256]{3,1,2,0:T(8,128)(2,1)S(1)}, f32[1,320,8,256]{3,1,2,0:T(8,128)}) fusion(bf16[1,320,1,256]{3,1,2,0:T(8,128)(2,1)S(1)} %collective-permute-done.5, bf16[1,320,8,256]{3,1,2,0:T(8,128)(2,1)S(1)} %get-tuple-element.247, bf16[3,3,320,320]{3,2,1,0:T(8,128)(2,1)S(1)} %copy-done.4, f32[8,256,320]{1,2,0:T(8,128)} %fusion.38, ...), kind=kOutput, calls=%fused_computation.36 | convolution fusion | flops 433848320 | bytes 29247488 | tf_op jit(solution)/shard_map/oi,tirw->torw/dot_general | solution.py:49
  113.2 4.5 %collective-permute-start.6 = (bf16[1,320,1,256]{3,1,2,0:T(8,128)(2,1)S(1)}, bf16[1,320,1,256]{3,1,2,0:T(8,128)(2,1)S(1)}, u32[]{:S(2)}, u32[]{:S(2)}) collective-permute-start(bf16[1,320,1,256]{3,1,2,0:T(8,128)(2,1)S(1)} %get-tuple-element.223), channel_id=1, source_target_pairs={{0,1},{1,2},{2,3},{3,4},{4,5},{5,6},{6,7},{8,9},{9,10},{10,11},{11... | collective-permute-start | bytes 491528 | tf_op jit(solution)/shard_map/ppermute | solution.py:14
  121.7 3.9 %collective-permute-done.7 = bf16[1,320,1,256]{3,1,2,0:T(8,128)(2,1)S(1)} collective-permute-done((bf16[1,320,1,256]{3,1,2,0:T(8,128)(2,1)S(1)}, bf16[1,320,1,256]{3,1,2,0:T(8,128)(2,1)S(1)}, u32[]{:S(2)}, u32[]{:S(2)}) %collective-permute-start.7) | collective-permute-done | bytes 163872 | tf_op jit(solution)/shard_map/ppermute | solution.py:17
  126.4 2.5 %fusion.126 = f32[8,256,320]{1,2,0:T(8,128)} fusion(bf16[1,320,8,255]{3,1,2,0:T(8,128)(2,1)S(1)} %get-tuple-element.220, bf16[3,3,320,320]{3,2,1,0:T(8,128)(2,1)S(1)} %copy-done.6), kind=kOutput, calls=%fused_computation.151 | convolution fusion | flops 419430400 | bytes 4177920 | tf_op jit(solution)/shard_map/oi,tirw->torw/dot_general | solution.py:49
  131.2 2.5 %fusion.132 = f32[8,256,320]{1,2,0:T(8,128)} fusion(bf16[1,320,8,255]{3,1,2,0:T(8,128)(2,1)S(1)} %get-tuple-element.222, bf16[3,3,320,320]{3,2,1,0:T(8,128)(2,1)S(1)} %copy-done.6), kind=kOutput, calls=%fused_computation.157 | convolution fusion | flops 419430400 | bytes 4177920 | tf_op jit(solution)/shard_map/oi,tirw->torw/dot_general | solution.py:49
  133.8 2.5 %fusion.134 = f32[8,256,320]{1,2,0:T(8,128)} fusion(bf16[1,320,8,255]{3,1,2,0:T(8,128)(2,1)S(1)} %get-tuple-element.219, bf16[3,3,320,320]{3,2,1,0:T(8,128)(2,1)S(1)} %copy-done.6), kind=kOutput, calls=%fused_computation.159 | convolution fusion | flops 419430400 | bytes 4177920 | tf_op jit(solution)/shard_map/oi,tirw->torw/dot_general | solution.py:49
  138.5 2.5 %fusion.95 = f32[8,256,320]{1,2,0:T(8,128)} fusion(bf16[1,320,8,256]{3,1,2,0:T(8,128)(2,1)S(1)} %get-tuple-element.249, bf16[1,320,1,256]{3,1,2,0:T(8,128)(2,1)S(1)} %collective-permute-done.6, bf16[3,3,320,320]{3,2,1,0:T(8,128)(2,1)S(1)} %copy-done.6), kind=kOutput, calls=%fused_computation.124 | convolution fusion | flops 424017920 | bytes 4341760 | tf_op jit(solution)/shard_map/oi,tirw->torw/dot_general | solution.py:49
  143.3 10.0 %fusion.203 = f32[1,16,8,256]{3,1,2,0:T(8,128)S(1)} fusion(f32[1,320,8,256]{3,1,2,0:T(8,128)} %get-tuple-element.250, f32[8,256,320]{1,2,0:T(8,128)} %fusion.28, f32[8,256,320]{1,2,0:T(8,128)} %fusion.126, f32[8,256,320]{1,2,0:T(8,128)} %fusion.128, f32[8,256,320]{1,2,0:T(8,128)} %fusion.130, f32[8,256,320]{1,2,0:T(8,128)} %fusion.132, ...), kind=kOutput, calls=%fused_computation.214 | convolution fusion | flops 454295552 | bytes 25717760 | tf_op jit(solution)/shard_map/cf,tfrw->tcrw/dot_general | solution.py:79
  153.4 7.0 %all_gather.7 = f32[4,16,8,256]{3,2,1,0:T(8,128)S(1)} all-gather(f32[1,16,8,256]{3,2,1,0:T(8,128)S(1)} %copy.24), channel_id=1, replica_groups=mesh['tm'=4,'space'=8] {'tm'}, dimensions={0}, use_global_device_ids=true | all-gather | bytes 655360 | tf_op jit(solution)/shard_map/all_gather | solution.py:24
  (76 shorter events, 55.0 us)
Async XLA Ops:
  0.0 1.6 %copy-start = (bf16[320,16]{0,1:T(8,128)(2,1)S(1)}, bf16[320,16]{0,1:T(8,128)(2,1)}, u32[]{:S(2)}) copy-start(bf16[320,16]{0,1:T(8,128)(2,1)} %param.16) | copy-start | bytes 30724
  4.0 10.9 %collective-permute-start = (bf16[1,320,1,256]{3,1,2,0:T(8,128)(2,1)S(1)}, bf16[1,320,1,256]{3,1,2,0:T(8,128)(2,1)S(1)}, u32[]{:S(2)}, u32[]{:S(2)}) collective-permute-start(bf16[1,320,1,256]{3,1,2,0:T(8,128)(2,1)S(1)} %get-tuple-element.241), channel_id=1, source_target_pairs={{0,1},{1,2},{2,3},{3,4},{4,5},{5,6},{6,7},{8,9},{9,10},{10,11},{11... | collective-permute-start | bytes 491528 | tf_op jit(solution)/shard_map/ppermute | solution.py:14
  8.9 7.6 %collective-permute-start.1 = (bf16[1,320,1,256]{3,1,2,0:T(8,128)(2,1)S(1)}, bf16[1,320,1,256]{3,1,2,0:T(8,128)(2,1)S(1)}, u32[]{:S(2)}, u32[]{:S(2)}) collective-permute-start(bf16[1,320,1,256]{3,1,2,0:T(8,128)(2,1)S(1)} %get-tuple-element.242), channel_id=1, source_target_pairs={{1,0},{2,1},{3,2},{4,3},{5,4},{6,5},{7,6},{9,8},{10,9},{11,10},{12... | collective-permute-start | bytes 491528 | tf_op jit(solution)/shard_map/ppermute | solution.py:17
  14.9 2.3 %copy-start.3 = (bf16[3,3,320,320]{3,2,1,0:T(8,128)(2,1)S(1)}, bf16[3,3,320,320]{3,2,1,0:T(8,128)(2,1)}, u32[]{:S(2)}) copy-start(bf16[3,3,320,320]{3,2,1,0:T(8,128)(2,1)} %param.17) | copy-start | bytes 5529604
  23.3 4.8 %copy-start.7 = (f32[8,256,320]{1,2,0:T(8,128)S(1)}, f32[8,256,320]{1,2,0:T(8,128)}, u32[]{:S(2)}) copy-start(f32[8,256,320]{1,2,0:T(8,128)} %get-tuple-element.244) | copy-start | bytes 7864324
  25.8 2.4 %copy-start.2 = (f32[8,256,320]{1,2,0:T(8,128)S(1)}, f32[8,256,320]{1,2,0:T(8,128)}, u32[]{:S(2)}) copy-start(f32[8,256,320]{1,2,0:T(8,128)} %fusion.160) | copy-start | bytes 7864324
  28.1 12.0 %copy-start.5 = (bf16[3,3,320,320]{3,2,1,0:T(8,128)(2,1)S(1)}, bf16[3,3,320,320]{3,2,1,0:T(8,128)(2,1)}, u32[]{:S(2)}) copy-start(bf16[3,3,320,320]{3,2,1,0:T(8,128)(2,1)} %param.18) | copy-start | bytes 5529604
  34.3 8.3 %collective-permute-start.2 = (bf16[1,320,1,256]{3,1,2,0:T(8,128)(2,1)S(1)}, bf16[1,320,1,256]{3,1,2,0:T(8,128)(2,1)S(1)}, u32[]{:S(2)}, u32[]{:S(2)}) collective-permute-start(bf16[1,320,1,256]{3,1,2,0:T(8,128)(2,1)S(1)} %get-tuple-element.235), channel_id=1, source_target_pairs={{0,1},{1,2},{2,3},{3,4},{4,5},{5,6},{6,7},{8,9},{9,10},{10,11},{11... | collective-permute-start | bytes 491528 | tf_op jit(solution)/shard_map/ppermute | solution.py:14
  38.7 7.8 %collective-permute-start.3 = (bf16[1,320,1,256]{3,1,2,0:T(8,128)(2,1)S(1)}, bf16[1,320,1,256]{3,1,2,0:T(8,128)(2,1)S(1)}, u32[]{:S(2)}, u32[]{:S(2)}) collective-permute-start(bf16[1,320,1,256]{3,1,2,0:T(8,128)(2,1)S(1)} %get-tuple-element.236), channel_id=1, source_target_pairs={{1,0},{2,1},{3,2},{4,3},{5,4},{6,5},{7,6},{9,8},{10,9},{11,10},{12... | collective-permute-start | bytes 491528 | tf_op jit(solution)/shard_map/ppermute | solution.py:17
  61.8 2.4 %copy-start.8 = (f32[16,8,256]{2,1,0:T(8,128)S(1)}, f32[16,8,256]{2,1,0:T(8,128)}, u32[]{:S(2)}) copy-start(f32[16,8,256]{2,1,0:T(8,128)} %param.12) | copy-start | bytes 393220
  61.8 2.4 %copy-start.9 = (bf16[16,320]{1,0:T(8,128)(2,1)S(1)}, bf16[16,320]{1,0:T(8,128)(2,1)}, u32[]{:S(2)}) copy-start(bf16[16,320]{1,0:T(8,128)(2,1)} %param.19) | copy-start | bytes 30724
  81.6 7.1 %copy-start.4 = (bf16[3,3,320,320]{3,2,1,0:T(8,128)(2,1)S(1)}, bf16[3,3,320,320]{3,2,1,0:T(8,128)(2,1)}, u32[]{:S(2)}) copy-start(bf16[3,3,320,320]{3,2,1,0:T(8,128)(2,1)} %param.17) | copy-start | bytes 5529604
  82.6 8.5 %collective-permute-start.4 = (bf16[1,320,1,256]{3,1,2,0:T(8,128)(2,1)S(1)}, bf16[1,320,1,256]{3,1,2,0:T(8,128)(2,1)S(1)}, u32[]{:S(2)}, u32[]{:S(2)}) collective-permute-start(bf16[1,320,1,256]{3,1,2,0:T(8,128)(2,1)S(1)} %get-tuple-element.229), channel_id=1, source_target_pairs={{0,1},{1,2},{2,3},{3,4},{4,5},{5,6},{6,7},{8,9},{9,10},{10,11},{11... | collective-permute-start | bytes 491528 | tf_op jit(solution)/shard_map/ppermute | solution.py:14
  87.2 8.2 %collective-permute-start.5 = (bf16[1,320,1,256]{3,1,2,0:T(8,128)(2,1)S(1)}, bf16[1,320,1,256]{3,1,2,0:T(8,128)(2,1)S(1)}, u32[]{:S(2)}, u32[]{:S(2)}) collective-permute-start(bf16[1,320,1,256]{3,1,2,0:T(8,128)(2,1)S(1)} %get-tuple-element.230), channel_id=1, source_target_pairs={{1,0},{2,1},{3,2},{4,3},{5,4},{6,5},{7,6},{9,8},{10,9},{11,10},{12... | collective-permute-start | bytes 491528 | tf_op jit(solution)/shard_map/ppermute | solution.py:17
  107.1 12.3 %copy-start.6 = (bf16[3,3,320,320]{3,2,1,0:T(8,128)(2,1)S(1)}, bf16[3,3,320,320]{3,2,1,0:T(8,128)(2,1)}, u32[]{:S(2)}) copy-start(bf16[3,3,320,320]{3,2,1,0:T(8,128)(2,1)} %param.18) | copy-start | bytes 5529604
  113.2 8.5 %collective-permute-start.6 = (bf16[1,320,1,256]{3,1,2,0:T(8,128)(2,1)S(1)}, bf16[1,320,1,256]{3,1,2,0:T(8,128)(2,1)S(1)}, u32[]{:S(2)}, u32[]{:S(2)}) collective-permute-start(bf16[1,320,1,256]{3,1,2,0:T(8,128)(2,1)S(1)} %get-tuple-element.223), channel_id=1, source_target_pairs={{0,1},{1,2},{2,3},{3,4},{4,5},{5,6},{6,7},{8,9},{9,10},{10,11},{11... | collective-permute-start | bytes 491528 | tf_op jit(solution)/shard_map/ppermute | solution.py:14
  117.8 7.9 %collective-permute-start.7 = (bf16[1,320,1,256]{3,1,2,0:T(8,128)(2,1)S(1)}, bf16[1,320,1,256]{3,1,2,0:T(8,128)(2,1)S(1)}, u32[]{:S(2)}, u32[]{:S(2)}) collective-permute-start(bf16[1,320,1,256]{3,1,2,0:T(8,128)(2,1)S(1)} %get-tuple-element.224), channel_id=1, source_target_pairs={{1,0},{2,1},{3,2},{4,3},{5,4},{6,5},{7,6},{9,8},{10,9},{11,10},{12... | collective-permute-start | bytes 491528 | tf_op jit(solution)/shard_map/ppermute | solution.py:17
  143.3 18.1 %copy-start.1 = (bf16[320,16]{0,1:T(8,128)(2,1)S(1)}, bf16[320,16]{0,1:T(8,128)(2,1)}, u32[]{:S(2)}) copy-start(bf16[320,16]{0,1:T(8,128)(2,1)} %param.16) | copy-start | bytes 30724
where the time goes:
time: 162 us; the launch traced here: 161 us
  matrix products  100 us (62%)
  starting transfers between devices  24.1 us (15%)
  waiting for transfers between devices  15.3 us (9%)
  blocking collectives  14.2 us (9%)
  other arithmetic  4.75 us (3%)
  between operations  1.62 us (1%)
    dot_general x34, matrix products, convolve(): jnp.einsum('oi,tirw->torw', weight[row_tap, col_tap], shift_columns(rows_...  77 us
    dot_general x2, matrix products, denoise(): jnp.einsum('cf,tfrw->tcrw', project_weight, active, preferred_element_typ...  20 us
    ppermute x4, starting transfers between devices, with_halo(): lax.ppermute(lax.slice_in_dim(block, block.shape[dim] - width, None, axis...  18.3 us
    all_gather x2, blocking collectives, prefix(): pieces = lax.all_gather(value, axis)  14.2 us
    ppermute x4, waiting for transfers between devices, with_halo(): lax.ppermute(lax.slice_in_dim(block, 0, width, axis=dim), axis, backward)  13.7 us
    ppermute x4, starting transfers between devices, with_halo(): lax.ppermute(lax.slice_in_dim(block, 0, width, axis=dim), axis, backward)  5.83 us
    dot_general x2, matrix products, denoise(): jnp.einsum('fc,tcrw->tfrw', lift_weight, states.astype(jnp.bfloat16), pre...  3.33 us
  transfers between devices with their start and end apart: 8, of which 5 were waited for; matrix products, arithmetic and copies ran while one was open for 6% of the time, Pallas kernels for 0%

commit v1 on v0

v1 whole, which is shorter than its diff:
```python
import functools

import jax
import jax.numpy as jnp
from jax import lax
from jax.experimental import pallas as pl
from jax.experimental.pallas import tpu as pltpu
from jax.sharding import PartitionSpec as P

ITERS = 2
MESH = pl.DeviceIdType.MESH


def silu(v):
    half = 0.5 * v
    return half + half * jnp.tanh(half)


def kernel(
    steps,
    tiles,
    x_ref,
    embed_ref,
    scale_ref,
    decay_ref,
    lift_ref,
    project_ref,
    conv_one_ref,
    conv_two_ref,
    out_ref,
    raw_one,
    raw_two,
    w_one,
    w_two,
    embed_bc,
    cols_one,
    cols_two,
    first,
    rows_f32,
    state_rows,
    xb_rows,
    halo_out,
    halo_in,
    drift_out,
    drift_in,
    w_sem,
    halo_send,
    halo_recv,
    drift_send,
    drift_recv,
):
    chans, height, width = x_ref.shape
    feats = lift_ref.shape[0]
    block = 3 * feats
    depth = 3 * block
    tm = lax.axis_index("tm")
    space = lax.axis_index("space")
    has_up = space > 0
    has_down = space < tiles - 1

    load_one = pltpu.make_async_copy(conv_one_ref, raw_one, w_sem.at[0])
    load_two = pltpu.make_async_copy(conv_two_ref, raw_two, w_sem.at[1])
    load_one.start()
    load_two.start()

    barrier = pltpu.get_barrier_semaphore()
    for shift in range(1, steps):
        other = lax.rem(tm + shift, steps)
        pl.semaphore_signal(barrier, inc=1, device_id=(other, space), device_id_type=MESH)

    @pl.when(has_up)
    def _():
        pl.semaphore_signal(barrier, inc=1, device_id=(tm, space - 1), device_id_type=MESH)

    @pl.when(has_down)
    def _():
        pl.semaphore_signal(barrier, inc=1, device_id=(tm, space + 1), device_id_type=MESH)

    def halo_copies(sweep):
        up = pltpu.make_async_remote_copy(
            src_ref=halo_out.at[sweep, 0],
            dst_ref=halo_in.at[sweep, 1],
            send_sem=halo_send.at[sweep, 0],
            recv_sem=halo_recv.at[sweep, 1],
            device_id=(tm, space - 1),
            device_id_type=MESH,
        )
        down = pltpu.make_async_remote_copy(
            src_ref=halo_out.at[sweep, 1],
            dst_ref=halo_in.at[sweep, 0],
            send_sem=halo_send.at[sweep, 1],
            recv_sem=halo_recv.at[sweep, 0],
            device_id=(tm, space + 1),
            device_id_type=MESH,
        )
        return up, down

    def send_halo(sweep):
        up, down = halo_copies(sweep)

        @pl.when(has_up)
        def _():
            up.start()

        @pl.when(has_down)
        def _():
            down.start()

    def wait_halo(sweep):
        up, down = halo_copies(sweep)

        @pl.when(has_up)
        def _():
            down.wait_recv()

        @pl.when(has_down)
        def _():
            up.wait_recv()

    def drift_copy(sweep, shift, row):
        return pltpu.make_async_remote_copy(
            src_ref=drift_out.at[sweep, row],
            dst_ref=drift_in.at[sweep, shift - 1, row],
            send_sem=drift_send.at[sweep, shift - 1, row],
            recv_sem=drift_recv.at[sweep, shift - 1, row],
            device_id=(tm + shift, space),
            device_id_type=MESH,
        )

    def send_drift(sweep, row):
        for shift in range(1, steps):

            @pl.when(tm + shift < steps)
            def _():
                drift_copy(sweep, shift, row).start()

    def earlier(sweep, row):
        total = jnp.zeros((chans, width), jnp.float32)
        for shift in range(1, steps):

            @pl.when(tm >= shift)
            def _():
                drift_copy(sweep, shift, row).wait_recv()

            total = total + jnp.where(tm >= shift, drift_in[sweep, shift - 1, row], 0.0)
        return total

    lane = lax.broadcasted_iota(jnp.int32, (feats, width), 1)

    def store_columns(cols, index, act):
        base = pl.multiple_of(index * block, 64)
        left = jnp.where(lane == 0, 0.0, pltpu.roll(act, 1, 1))
        right = jnp.where(lane == width - 1, 0.0, pltpu.roll(act, width - 1, 1))
        cols[pl.ds(base, feats), :] = left.astype(jnp.bfloat16)
        cols[pl.ds(base + feats, feats), :] = act.astype(jnp.bfloat16)
        cols[pl.ds(base + 2 * feats, feats), :] = right.astype(jnp.bfloat16)

    def lift(xb):
        value = jnp.dot(lift_ref[...], xb, preferred_element_type=jnp.float32)
        return value + jnp.concatenate([embed_bc[...]] * (width // 128), axis=1)

    def conv(weight, cols, index):
        base = pl.multiple_of(index * block, 64)
        return jnp.dot(
            weight[...], cols[pl.ds(base, depth), :], preferred_element_type=jnp.float32
        )

    def own_row(row):
        lifted = lift(xb_rows[row])
        first[row + 1] = lifted
        store_columns(cols_one, row + 2, silu(lifted))

    def halo_row(sweep, side, step):
        inside = has_up if side == 0 else has_down
        lifted = lift(jnp.where(inside, halo_in[sweep, side, step], 0))
        if side == 0 and step == 1:
            first[0] = lifted
        if side == 1 and step == 0:
            first[height + 1] = lifted
        index = step if side == 0 else height + 2 + step
        store_columns(cols_one, index, jnp.where(inside, silu(lifted), 0.0))

    def conv_one_row(index, inside=None):
        value = first[index] + conv(w_one, cols_one, index)
        first[index] = value
        act = silu(value)
        if inside is not None:
            act = jnp.where(inside, act, 0.0)
        store_columns(cols_two, index, act)

    def conv_two_row(sweep, row):
        value = first[row + 1] + conv(w_two, cols_two, row)
        act = silu(value).astype(jnp.bfloat16)
        out = jnp.dot(project_ref[...], act, preferred_element_type=jnp.float32)
        drift_out[sweep, row] = scale_ref[0] * out - decay_ref[0] * state_rows[row]
        send_drift(sweep, row)

    def build_weight(raw, weight):
        for tap in range(9):
            weight[:, tap * feats : (tap + 1) * feats] = raw[tap // 3, tap % 3]

    for row in range(height):
        value = x_ref[:, row, :]
        rows_f32[row] = value
        state_rows[row] = value
        rounded = value.astype(jnp.bfloat16)
        xb_rows[row] = rounded
        if row < 2:
            halo_out[0, 0, row] = rounded
        if row >= height - 2:
            halo_out[0, 1, row - (height - 2)] = rounded
    embed_bc[...] = jnp.transpose(
        jnp.pad(jnp.broadcast_to(embed_ref[...], (128, feats)), ((0, 0), (0, (-feats) % 128)))
    )[:feats]

    greeted = (steps - 1) + jnp.where(has_up, 1, 0) + jnp.where(has_down, 1, 0)
    pl.semaphore_wait(barrier, greeted)
    send_halo(0)

    for sweep in range(ITERS):
        if sweep > 0:
            for row in (0, 1, height - 1, height - 2):
                state = rows_f32[row] + earlier(sweep - 1, row)
                state_rows[row] = state
                rounded = state.astype(jnp.bfloat16)
                xb_rows[row] = rounded
                if row < 2:
                    halo_out[sweep, 0, row] = rounded
                else:
                    halo_out[sweep, 1, row - (height - 2)] = rounded
            send_halo(sweep)

            @pl.loop(2, height - 2)
            def _(row):
                state = rows_f32[row] + earlier(sweep - 1, row)
                state_rows[row] = state
                xb_rows[row] = state.astype(jnp.bfloat16)

        @pl.loop(0, height)
        def _(row):
            own_row(row)

        if sweep == 0:
            load_one.wait()
            build_weight(raw_one, w_one)

        @pl.loop(2, height)
        def _(index):
            conv_one_row(index)

        wait_halo(sweep)
        for side in range(2):
            for step in range(2):
                halo_row(sweep, side, step)
        conv_one_row(1)
        conv_one_row(height)
        conv_one_row(0, has_up)
        conv_one_row(height + 1, has_down)

        if sweep == 0:
            load_two.wait()
            build_weight(raw_two, w_two)

        @pl.loop(0, height)
        def _(turn):
            row = jnp.where(turn < 2, turn, jnp.where(turn < 4, height + 1 - turn, turn - 2))
            conv_two_row(sweep, row)

    for row in range(height):
        total = drift_out[ITERS - 1, row] + earlier(ITERS - 1, row)
        out_ref[0, :, row, :] = rows_f32[row] + total

    for sweep in range(ITERS):
        up, down = halo_copies(sweep)

        @pl.when(has_up)
        def _():
            up.wait_send()

        @pl.when(has_down)
        def _():
            down.wait_send()

        for shift in range(1, steps):
            for row in range(height):

                @pl.when(tm + shift < steps)
                def _():
                    drift_copy(sweep, shift, row).wait_send()


def solution(mesh):
    steps, tiles = mesh.shape["tm"], mesh.shape["space"]

    def per_device(
        first_state,
        time_embed,
        drift_scale,
        state_decay,
        lift_weight,
        conv_one,
        conv_two,
        project_weight,
    ):
        chans, height, width = first_state.shape
        feats = lift_weight.shape[0]
        block, depth = 3 * feats, 9 * feats
        peers = max(steps - 1, 1)
        vmem = pl.BlockSpec(memory_space=pltpu.VMEM)
        smem = pl.BlockSpec(memory_space=pltpu.SMEM)
        hbm = pl.BlockSpec(memory_space=pl.ANY)
        return pl.pallas_call(
            functools.partial(kernel, steps, tiles),
            out_shape=jax.ShapeDtypeStruct((1, chans, height, width), jnp.float32),
            in_specs=[vmem, vmem, smem, smem, vmem, vmem, hbm, hbm],
            out_specs=vmem,
            scratch_shapes=[
                pltpu.VMEM((3, 3, feats, feats), jnp.bfloat16),
                pltpu.VMEM((3, 3, feats, feats), jnp.bfloat16),
                pltpu.VMEM((feats, depth), jnp.bfloat16),
                pltpu.VMEM((feats, depth), jnp.bfloat16),
                pltpu.VMEM((feats, 128), jnp.float32),
                pltpu.VMEM(((height + 4) * block, width), jnp.bfloat16),
                pltpu.VMEM(((height + 2) * block, width), jnp.bfloat16),
                pltpu.VMEM((height + 2, feats, width), jnp.float32),
                pltpu.VMEM((height, chans, width), jnp.float32),
                pltpu.VMEM((height, chans, width), jnp.float32),
                pltpu.VMEM((height, chans, width), jnp.bfloat16),
                pltpu.VMEM((ITERS, 2, 2, chans, width), jnp.bfloat16),
                pltpu.VMEM((ITERS, 2, 2, chans, width), jnp.bfloat16),
                pltpu.VMEM((ITERS, height, chans, width), jnp.float32),
                pltpu.VMEM((ITERS, peers, height, chans, width), jnp.float32),
                pltpu.SemaphoreType.DMA((2,)),
                pltpu.SemaphoreType.DMA((ITERS, 2)),
                pltpu.SemaphoreType.DMA((ITERS, 2)),
                pltpu.SemaphoreType.DMA((ITERS, peers, height)),
                pltpu.SemaphoreType.DMA((ITERS, peers, height)),
            ],
            compiler_params=pltpu.CompilerParams(
                collective_id=0, has_side_effects=True, vmem_limit_bytes=48 * 1024 * 1024
            ),
        )(
            first_state,
            time_embed,
            drift_scale,
            state_decay,
            lift_weight,
            project_weight,
            conv_one,
            conv_two,
        )

    in_specs = (P(None, "space", None), P("tm", None), P("tm"), P("tm"), P(), P(), P(), P())
    return jax.shard_map(
        per_device,
        mesh=mesh,
        in_specs=in_specs,
        out_specs=P("tm", None, "space", None),
        check_vma=False,
    )
```

time: 162 us -> 49.8 us (0.31)
  matrix products: 100 us -> 0 us
  Pallas kernels: 0 us -> 40.6 us
  starting transfers between devices: 24.1 us -> 0 us
  waiting for transfers between devices: 15.3 us -> 0 us
  blocking collectives: 14.2 us -> 0 us
  local copies, waits for them, and re-layouts: 1.03 us -> 7.02 us
  other arithmetic: 4.75 us -> 0 us
    dot_general x38 -> x0, matrix products: 100 us -> none  [the longest x34 77 us: convolve(): jnp.einsum('oi,tirw->torw', weight[row_tap, col_tap], shift_columns(rows_...]
    pallas_call x0 -> x1, Pallas kernels: none -> 40.6 us  [per_device(): pl.pallas_call(functools.partial(kernel, steps, tiles), out_shape=jax.Sha...]
    ppermute x8 -> x0, starting transfers between devices: 24.1 us -> none  [the longest x4 18.3 us: with_halo(): lax.ppermute(lax.slice_in_dim(block, block.shape[dim] - width, None, axis...]
    ppermute x8 -> x0, waiting for transfers between devices: 15.3 us -> none  [the longest x4 13.7 us: with_halo(): lax.ppermute(lax.slice_in_dim(block, 0, width, axis=dim), axis, backward)]
    all_gather x2 -> x0, blocking collectives: 14.2 us -> none  [prefix(): pieces = lax.all_gather(value, axis)]
    unnamed x20 -> x12, local copies, waits for them, and re-layouts: 0.04 us -> 7.02 us
    concatenate x4 -> x0, other arithmetic: 2.79 us -> none  [with_halo(): block = jnp.concatenate([low, block, high], axis=dim)]
  transfers between devices with their start and end apart: 8 -> 0, of which waited for: 5 -> 0; matrix products, arithmetic and copies ran while one was open for 6% -> 0% of each run, Pallas kernels for 0% -> 0%
where the time goes in v1:
time: 49.8 us; the launch traced here: 48.9 us
  Pallas kernels  40.6 us (82%)
  local copies, waits for them, and re-layouts  7.02 us (14%)
  between operations  1.32 us (3%)
    pallas_call x1, Pallas kernels, per_device(): pl.pallas_call(functools.partial(kernel, steps, tiles), out_shape=jax.Sha...  40.6 us
    unnamed x12, local copies, waits for them, and re-layouts  7.02 us

profile of v1, /device:TPU:0, one launch (start us, length us, event | category | flops | bytes accessed | tf_op | source)
XLA Modules:
  0.0 48.9 jit_solution(3635411436020995534)
XLA Ops:
  1.3 0.8 %copy.9.lift_ref = bf16[320,16]{1,0:T(8,128)(2,1)S(1)} copy(bf16[320,16]{0,1:T(8,128)(2,1)} %param.12) | data formatting | bytes 20480 | tf_op args[4]
  2.1 0.0 copy-start
  2.1 1.6 %copy-done = bf16[3,3,320,320]{3,2,1,0:T(8,128)(2,1)S(1)} copy-done((bf16[3,3,320,320]{3,2,1,0:T(8,128)(2,1)S(1)}, bf16[3,3,320,320]{3,2,1,0:T(8,128)(2,1)}, u32[]{:S(2)}) %copy-start) | copy-done | bytes 1843224
  3.8 0.0 copy-start.1
  3.8 1.6 %copy-done.1 = bf16[3,3,320,320]{3,2,1,0:T(8,128)(2,1)S(1)} copy-done((bf16[3,3,320,320]{3,2,1,0:T(8,128)(2,1)S(1)}, bf16[3,3,320,320]{3,2,1,0:T(8,128)(2,1)}, u32[]{:S(2)}) %copy-start.1) | copy-done | bytes 1843224
  5.4 0.0 copy-start.2
  5.4 0.9 %copy-done.2 = f32[16,8,256]{2,1,0:T(8,128)S(1)} copy-done((f32[16,8,256]{2,1,0:T(8,128)S(1)}, f32[16,8,256]{2,1,0:T(8,128)}, u32[]{:S(2)}) %copy-start.2) | copy-done | bytes 131096
  6.3 0.0 copy-start.3
  6.3 0.7 %copy-done.3 = bf16[16,320]{1,0:T(8,128)(2,1)S(1)} copy-done((bf16[16,320]{1,0:T(8,128)(2,1)S(1)}, bf16[16,320]{1,0:T(8,128)(2,1)}, u32[]{:S(2)}) %copy-start.3) | copy-done | bytes 10264
  7.0 0.0 copy-start.4
  7.0 0.7 %copy-done.4 = f32[1,320]{1,0:T(1,128)S(1)} copy-done((f32[1,320]{1,0:T(1,128)S(1)}, f32[1,320]{1,0:T(1,128)}, u32[]{:S(2)}) %copy-start.4) | copy-done | bytes 1304
  7.7 40.6 %shard_map.82 = f32[1,16,8,256]{3,2,1,0:T(8,128)S(1)} custom-call(f32[16,8,256]{2,1,0:T(8,128)S(1)} %copy-done.2, f32[1,320]{1,0:T(1,128)S(1)} %copy-done.4, f32[1]{0:T(128)S(6)} %copy.11.scale_ref, f32[1]{0:T(128)S(6)} %copy.12.decay_ref, bf16[320,16]{1,0:T(8,128)(2,1)S(1)} %copy.9.lift_ref, bf16[16,320]{1,0:T(8,128)(2,1)S(1)} %copy-done.3, ...), custom_call_target="tpu_custom_call" | custom-call | tf_op jit(solution)/shard_map/pallas_call | solution.py:312
  48.3 0.7 %copy.13 = f32[1,16,8,256]{3,2,1,0:T(8,128)} copy(f32[1,16,8,256]{3,2,1,0:T(8,128)S(1)} %shard_map.82) | data formatting | bytes 262144
Async XLA Ops:
  2.1 1.6 %copy-start = (bf16[3,3,320,320]{3,2,1,0:T(8,128)(2,1)S(1)}, bf16[3,3,320,320]{3,2,1,0:T(8,128)(2,1)}, u32[]{:S(2)}) copy-start(bf16[3,3,320,320]{3,2,1,0:T(8,128)(2,1)} %conv_one_ref.1) | copy-start | bytes 5529604
  3.8 1.6 %copy-start.1 = (bf16[3,3,320,320]{3,2,1,0:T(8,128)(2,1)S(1)}, bf16[3,3,320,320]{3,2,1,0:T(8,128)(2,1)}, u32[]{:S(2)}) copy-start(bf16[3,3,320,320]{3,2,1,0:T(8,128)(2,1)} %conv_two_ref.1) | copy-start | bytes 5529604
  5.4 0.9 %copy-start.2 = (f32[16,8,256]{2,1,0:T(8,128)S(1)}, f32[16,8,256]{2,1,0:T(8,128)}, u32[]{:S(2)}) copy-start(f32[16,8,256]{2,1,0:T(8,128)} %x_ref.1) | copy-start | bytes 393220
  6.3 0.7 %copy-start.3 = (bf16[16,320]{1,0:T(8,128)(2,1)S(1)}, bf16[16,320]{1,0:T(8,128)(2,1)}, u32[]{:S(2)}) copy-start(bf16[16,320]{1,0:T(8,128)(2,1)} %project_ref.1) | copy-start | bytes 30724
  7.0 0.7 %copy-start.4 = (f32[1,320]{1,0:T(1,128)S(1)}, f32[1,320]{1,0:T(1,128)}, u32[]{:S(2)}) copy-start(f32[1,320]{1,0:T(1,128)} %embed_ref.1) | copy-start | bytes 3844

commit v2 on v1

v2 whole, which is shorter than its diff:
```python
import functools

import jax
import jax.numpy as jnp
from jax import lax
from jax.experimental import pallas as pl
from jax.experimental.pallas import tpu as pltpu
from jax.sharding import PartitionSpec as P

ITERS = 2
MESH = pl.DeviceIdType.MESH


def silu(v):
    half = 0.5 * v
    return half + half * jnp.tanh(half)


def kernel(
    steps,
    tiles,
    x_hbm,
    embed_hbm,
    scale_ref,
    decay_ref,
    lift_hbm,
    project_hbm,
    conv_one_hbm,
    conv_two_hbm,
    out_ref,
    x_ref,
    embed_ref,
    lift_ref,
    project_ref,
    raw_one,
    raw_two,
    w_one,
    w_two,
    embed_bc,
    lift_rows,
    cols_one,
    cols_two,
    first,
    sums_one,
    sums_two,
    act_three,
    rows_f32,
    state_rows,
    xb_rows,
    drift_out,
    drift_in,
    load_sem,
    halo_send,
    halo_recv,
    drift_send,
    drift_recv,
):
    chans, height, width = x_ref.shape
    feats = lift_ref.shape[1]
    block = 3 * feats
    depth = 3 * block
    chunk = 64 if feats % 64 == 0 else feats
    tm = lax.axis_index("tm")
    space = lax.axis_index("space")
    has_up = space > 0
    has_down = space < tiles - 1

    pairs = (
        (x_hbm, x_ref),
        (embed_hbm, embed_ref),
        (lift_hbm, lift_ref),
        (project_hbm, project_ref),
        (conv_one_hbm, raw_one),
        (conv_two_hbm, raw_two),
    )
    loads = [pltpu.make_async_copy(a, b, load_sem.at[i]) for i, (a, b) in enumerate(pairs)]
    for load in loads:
        load.start()

    barrier = pltpu.get_barrier_semaphore()
    for shift in range(1, steps):
        other = lax.rem(tm + shift, steps)
        pl.semaphore_signal(barrier, inc=1, device_id=(other, space), device_id_type=MESH)

    @pl.when(has_up)
    def _():
        pl.semaphore_signal(barrier, inc=1, device_id=(tm, space - 1), device_id_type=MESH)

    @pl.when(has_down)
    def _():
        pl.semaphore_signal(barrier, inc=1, device_id=(tm, space + 1), device_id_type=MESH)

    def halo_copies(sweep):
        up = pltpu.make_async_remote_copy(
            src_ref=xb_rows.at[sweep, pl.ds(2, 2)],
            dst_ref=xb_rows.at[sweep, pl.ds(height + 2, 2)],
            send_sem=halo_send.at[sweep, 0],
            recv_sem=halo_recv.at[sweep, 1],
            device_id=(tm, space - 1),
            device_id_type=MESH,
        )
        down = pltpu.make_async_remote_copy(
            src_ref=xb_rows.at[sweep, pl.ds(height, 2)],
            dst_ref=xb_rows.at[sweep, pl.ds(0, 2)],
            send_sem=halo_send.at[sweep, 1],
            recv_sem=halo_recv.at[sweep, 0],
            device_id=(tm, space + 1),
            device_id_type=MESH,
        )
        return up, down

    def send_halo(sweep):
        up, down = halo_copies(sweep)

        @pl.when(has_up)
        def _():
            up.start()

        @pl.when(has_down)
        def _():
            down.start()

    def wait_halo(sweep):
        up, down = halo_copies(sweep)

        @pl.when(has_up)
        def _():
            down.wait_recv()

        @pl.when(has_down)
        def _():
            up.wait_recv()

    def drift_copy(sweep, shift, row):
        return pltpu.make_async_remote_copy(
            src_ref=drift_out.at[sweep, row],
            dst_ref=drift_in.at[sweep, shift - 1, row],
            send_sem=drift_send.at[sweep, shift - 1, row],
            recv_sem=drift_recv.at[sweep, shift - 1, row],
            device_id=(tm + shift, space),
            device_id_type=MESH,
        )

    def send_drift(sweep, row):
        for shift in range(1, steps):

            @pl.when(tm + shift < steps)
            def _():
                drift_copy(sweep, shift, row).start()

    def earlier(sweep, row):
        total = jnp.zeros((chans, width), jnp.float32)
        for shift in range(1, steps):

            @pl.when(tm >= shift)
            def _():
                drift_copy(sweep, shift, row).wait_recv()

            total = total + jnp.where(tm >= shift, drift_in[sweep, shift - 1, row], 0.0)
        return total

    lane = lax.broadcasted_iota(jnp.int32, (chunk, width), 1)
    zero = jnp.zeros((), jnp.bfloat16)

    def store_columns(cols, index, start, act):
        base = index * block + start
        mid = act.astype(jnp.bfloat16)
        left = jnp.where(lane == 0, zero, pltpu.roll(mid, 1, 1))
        right = jnp.where(lane == width - 1, zero, pltpu.roll(mid, width - 1, 1))
        cols[base : base + chunk, :] = left
        cols[base + feats : base + feats + chunk, :] = mid
        cols[base + 2 * feats : base + 2 * feats + chunk, :] = right

    def build(sweep, index):
        inside = None
        if index < 2:
            inside = has_up
        if index >= height + 2:
            inside = has_down
        xb = xb_rows[sweep, index]
        for start in range(0, feats, chunk):
            lifted = jnp.dot(
                lift_rows[start : start + chunk, :chans], xb, preferred_element_type=jnp.float32
            )
            lifted = lifted + jnp.concatenate(
                [embed_bc[start : start + chunk, :]] * (width // 128), axis=1
            )
            if 1 <= index <= height + 2:
                first[index - 1, start : start + chunk, :] = lifted
            act = silu(lifted)
            if inside is not None:
                act = jnp.where(inside, act, 0.0)
            store_columns(cols_one, index, start, act)

    def conv(weight, cols, index):
        return jnp.dot(
            weight[...],
            cols[index * block : index * block + depth, :],
            preferred_element_type=jnp.float32,
        )

    def activate_one(index):
        inside = None
        if index == 0:
            inside = has_up
        if index == height + 1:
            inside = has_down
        for start in range(0, feats, chunk):
            act = silu(sums_one[index % 2, start : start + chunk, :])
            if inside is not None:
                act = jnp.where(inside, act, 0.0)
            store_columns(cols_two, index, start, act)

    def finish_row(sweep, row):
        for start in range(0, feats, chunk):
            act = silu(sums_two[row % 2, start : start + chunk, :])
            act_three[row % 2, start : start + chunk, :] = act.astype(jnp.bfloat16)
        out = jnp.dot(project_ref[...], act_three[row % 2], preferred_element_type=jnp.float32)
        drift_out[sweep, row] = scale_ref[0] * out - decay_ref[0] * state_rows[row]

    def build_weight(raw, weight):
        for tap in range(9):
            weight[:, tap * feats : (tap + 1) * feats] = raw[tap // 3, tap % 3]

    def take_state(sweep, row):
        state = rows_f32[row] + earlier(sweep - 1, row)
        state_rows[row] = state
        xb_rows[sweep, row + 2] = state.astype(jnp.bfloat16)

    def one_sweep(sweep):
        edges = (0, 1, height - 1, height - 2)

        @pl.when(sweep > 0)
        def _():
            for row in edges:
                take_state(sweep, row)
            send_halo(sweep)
            take_state(sweep, 2)

        for index in (2, 3, 4):
            build(sweep, index)

        @pl.when(sweep == 0)
        def _():
            loads[4].wait()
            build_weight(raw_one, w_one)

        order = list(range(2, height)) + [1, height, 0, height + 1]
        builds = list(range(5, height + 2)) + [1, height + 2, 0, height + 3]
        before = None
        for turn, index in enumerate(order):
            fresh = builds[turn] if turn < len(builds) else None
            if fresh is not None and 5 <= fresh < height:

                @pl.when(sweep > 0)
                def _():
                    take_state(sweep, fresh - 2)

            if fresh == 1:
                wait_halo(sweep)
            value = first[index] + conv(w_one, cols_one, index)
            if fresh is not None:
                build(sweep, fresh)
            if before is not None:
                activate_one(before)
            first[index] = value
            sums_one[index % 2] = value
            before = index

        @pl.when(sweep == 0)
        def _():
            loads[5].wait()
            build_weight(raw_two, w_two)

        done = None
        for row in edges + tuple(range(2, height - 2)):
            value = first[row + 1] + conv(w_two, cols_two, row)
            if done is None:
                activate_one(before)
            else:
                finish_row(sweep, done)
            sums_two[row % 2] = value
            if done is not None:
                send_drift(sweep, done)
            done = row
        finish_row(sweep, done)
        send_drift(sweep, done)

    loads[0].wait()
    for row in range(height):
        value = x_ref[:, row, :]
        rows_f32[row] = value
        state_rows[row] = value
        xb_rows[0, row + 2] = value.astype(jnp.bfloat16)
    greeted = (steps - 1) + jnp.where(has_up, 1, 0) + jnp.where(has_down, 1, 0)
    pl.semaphore_wait(barrier, greeted)
    send_halo(0)
    for load in loads[1:4]:
        load.wait()
    wide = (-feats) % 128
    embed_bc[...] = jnp.transpose(
        jnp.pad(jnp.broadcast_to(embed_ref[...], (128, feats)), ((0, 0), (0, wide)))
    )[:feats]
    turned = jnp.transpose(
        jnp.pad(lift_ref[...].astype(jnp.float32), ((0, 128 - chans), (0, wide)))
    )[:feats]
    lift_rows[...] = turned.astype(jnp.bfloat16)

    @pl.loop(0, ITERS)
    def _(sweep):
        one_sweep(sweep)

    for row in range(height):
        total = drift_out[ITERS - 1, row] + earlier(ITERS - 1, row)
        out_ref[0, :, row, :] = rows_f32[row] + total

    for sweep in range(ITERS):
        up, down = halo_copies(sweep)

        @pl.when(has_up)
        def _():
            up.wait_send()

        @pl.when(has_down)
        def _():
            down.wait_send()

        for shift in range(1, steps):
            for row in range(height):

                @pl.when(tm + shift < steps)
                def _():
                    drift_copy(sweep, shift, row).wait_send()


def solution(mesh):
    steps, tiles = mesh.shape["tm"], mesh.shape["space"]

    def per_device(
        first_state,
        time_embed,
        drift_scale,
        state_decay,
        lift_weight,
        conv_one,
        conv_two,
        project_weight,
    ):
        chans, height, width = first_state.shape
        feats = lift_weight.shape[0]
        block, depth = 3 * feats, 9 * feats
        peers = max(steps - 1, 1)
        vmem = pl.BlockSpec(memory_space=pltpu.VMEM)
        smem = pl.BlockSpec(memory_space=pltpu.SMEM)
        hbm = pl.BlockSpec(memory_space=pl.ANY)
        return pl.pallas_call(
            functools.partial(kernel, steps, tiles),
            out_shape=jax.ShapeDtypeStruct((1, chans, height, width), jnp.float32),
            in_specs=[hbm, hbm, smem, smem, hbm, hbm, hbm, hbm],
            out_specs=vmem,
            scratch_shapes=[
                pltpu.VMEM((chans, height, width), jnp.float32),
                pltpu.VMEM((1, feats), jnp.float32),
                pltpu.VMEM((chans, feats), jnp.bfloat16),
                pltpu.VMEM((chans, feats), jnp.bfloat16),
                pltpu.VMEM((3, 3, feats, feats), jnp.bfloat16),
                pltpu.VMEM((3, 3, feats, feats), jnp.bfloat16),
                pltpu.VMEM((feats, depth), jnp.bfloat16),
                pltpu.VMEM((feats, depth), jnp.bfloat16),
                pltpu.VMEM((feats, 128), jnp.float32),
                pltpu.VMEM((feats, 128), jnp.bfloat16),
                pltpu.VMEM(((height + 4) * block, width), jnp.bfloat16),
                pltpu.VMEM(((height + 2) * block, width), jnp.bfloat16),
                pltpu.VMEM((height + 2, feats, width), jnp.float32),
                pltpu.VMEM((2, feats, width), jnp.float32),
                pltpu.VMEM((2, feats, width), jnp.float32),
                pltpu.VMEM((2, feats, width), jnp.bfloat16),
                pltpu.VMEM((height, chans, width), jnp.float32),
                pltpu.VMEM((height, chans, width), jnp.float32),
                pltpu.VMEM((ITERS, height + 4, chans, width), jnp.bfloat16),
                pltpu.VMEM((ITERS, height, chans, width), jnp.float32),
                pltpu.VMEM((ITERS, peers, height, chans, width), jnp.float32),
                pltpu.SemaphoreType.DMA((6,)),
                pltpu.SemaphoreType.DMA((ITERS, 2)),
                pltpu.SemaphoreType.DMA((ITERS, 2)),
                pltpu.SemaphoreType.DMA((ITERS, peers, height)),
                pltpu.SemaphoreType.DMA((ITERS, peers, height)),
            ],
            compiler_params=pltpu.CompilerParams(
                collective_id=0, has_side_effects=True, vmem_limit_bytes=67043328
            ),
        )(
            first_state,
            time_embed,
            drift_scale,
            state_decay,
            lift_weight.T,
            project_weight,
            conv_one,
            conv_two,
        )

    in_specs = (P(None, "space", None), P("tm", None), P("tm"), P("tm"), P(), P(), P(), P())
    return jax.shard_map(
        per_device,
        mesh=mesh,
        in_specs=in_specs,
        out_specs=P("tm", None, "space", None),
        check_vma=False,
    )
```

time: 49.8 us -> 45.6 us (0.916); the launches traced: 48.9 us -> 45.4 us
  local copies, waits for them, and re-layouts: 7.02 us -> 1.57 us
  Pallas kernels: 40.6 us -> 42.5 us
    unnamed x12 -> x1, local copies, waits for them, and re-layouts: 7.02 us -> 1.57 us
    pallas_call x1, Pallas kernels: 40.6 us -> 42.5 us  [per_device(): pl.pallas_call(functools.partial(kernel, steps, tiles), out_shape=jax.Sha...]
where the time goes in v2:
time: 45.6 us; the launch traced here: 45.4 us
  Pallas kernels  42.5 us (93%)
  local copies, waits for them, and re-layouts  1.57 us (3%)
  between operations  1.3 us (3%)
    pallas_call x1, Pallas kernels, per_device(): pl.pallas_call(functools.partial(kernel, steps, tiles), out_shape=jax.Sha...  42.5 us
    unnamed x1, local copies, waits for them, and re-layouts  1.57 us

profile of v2, /device:TPU:0, one launch (start us, length us, event | category | flops | bytes accessed | tf_op | source)
XLA Modules:
  0.0 45.4 jit_solution(11229676170759777498)
XLA Ops:
  1.3 42.5 %shard_map.82 = f32[1,16,8,256]{3,2,1,0:T(8,128)} custom-call(f32[16,8,256]{2,1,0:T(8,128)} %x_hbm.1, f32[1,320]{1,0:T(1,128)} %embed_hbm.1, f32[1]{0:T(128)S(6)} %copy.10.scale_ref, f32[1]{0:T(128)S(6)} %copy.11.decay_ref, bf16[16,320]{1,0:T(8,128)(2,1)} %bitcast.1, bf16[16,320]{1,0:T(8,128)(2,1)} %project_hbm.1, bf16[3,3,320,320]{3,2,1,0:T(8,128)(2,1)} %conv_one_hbm.1, ...), custom_call_target="tpu_custom_call" | custom-call | tf_op jit(solution)/shard_map/pallas_call | solution.py:356
  43.8 1.6 %copy.12 = f32[1,16,8,256]{3,2,1,0:T(8,128)} copy(f32[1,16,8,256]{3,2,1,0:T(8,128)} %shard_map.82) | data formatting | bytes 262144

commit v3 on v2

--- a/solution.py
+++ b/solution.py
@@ -192,31 +192,35 @@
                 act = jnp.where(inside, act, 0.0)
             store_columns(cols_one, index, start, act)
 
-    def conv(weight, cols, index):
+    def conv_pair(weight, cols, pair):
+        taken = [cols[index * block : index * block + depth, :] for index in pair]
         return jnp.dot(
-            weight[...],
-            cols[index * block : index * block + depth, :],
-            preferred_element_type=jnp.float32,
+            weight[...], jnp.concatenate(taken, axis=1), preferred_element_type=jnp.float32
         )
 
-    def activate_one(index):
+    def activate_one(index, slot):
         inside = None
         if index == 0:
             inside = has_up
         if index == height + 1:
             inside = has_down
         for start in range(0, feats, chunk):
-            act = silu(sums_one[index % 2, start : start + chunk, :])
+            act = silu(sums_one[slot, start : start + chunk, :])
             if inside is not None:
                 act = jnp.where(inside, act, 0.0)
             store_columns(cols_two, index, start, act)
 
-    def finish_row(sweep, row):
+    def finish_pair(sweep, pair, slot):
         for start in range(0, feats, chunk):
-            act = silu(sums_two[row % 2, start : start + chunk, :])
-            act_three[row % 2, start : start + chunk, :] = act.astype(jnp.bfloat16)
-        out = jnp.dot(project_ref[...], act_three[row % 2], preferred_element_type=jnp.float32)
-        drift_out[sweep, row] = scale_ref[0] * out - decay_ref[0] * state_rows[row]
+            for half in range(2):
+                act = silu(sums_two[slot + half, start : start + chunk, :])
+                act_three[
+                    slot // 2, start : start + chunk, half * width : (half + 1) * width
+                ] = act.astype(jnp.bfloat16)
+        out = jnp.dot(project_ref[...], act_three[slot // 2], preferred_element_type=jnp.float32)
+        for half, row in enumerate(pair):
+            part = out[:, half * width : (half + 1) * width]
+            drift_out[sweep, row] = scale_ref[0] * part - decay_ref[0] * state_rows[row]
 
     def build_weight(raw, weight):
         for tap in range(9):
@@ -229,6 +233,7 @@
 
     def one_sweep(sweep):
         edges = (0, 1, height - 1, height - 2)
+        middle = tuple(range(2, height - 2))
 
         @pl.when(sweep > 0)
         def _():
@@ -236,8 +241,9 @@
                 take_state(sweep, row)
             send_halo(sweep)
             take_state(sweep, 2)
-
-        for index in (2, 3, 4):
+            take_state(sweep, 3)
+
+        for index in (2, 3, 4, 5):
             build(sweep, index)
 
         @pl.when(sweep == 0)
@@ -245,46 +251,62 @@
             loads[4].wait()
             build_weight(raw_one, w_one)
 
-        order = list(range(2, height)) + [1, height, 0, height + 1]
-        builds = list(range(5, height + 2)) + [1, height + 2, 0, height + 3]
+        order = [(index, index + 1) for index in range(2, height, 2)]
+        order += [(1, height), (0, height + 1)]
+        builds = [(index + 4, index + 5) for index in range(2, height - 2, 2)]
+        builds += [(1, height + 2), (0, height + 3), ()]
         before = None
-        for turn, index in enumerate(order):
-            fresh = builds[turn] if turn < len(builds) else None
-            if fresh is not None and 5 <= fresh < height:
+        for turn, pair in enumerate(order):
+            fresh = builds[turn]
+            late = [index - 2 for index in fresh if 6 <= index < height]
+            if late:
 
                 @pl.when(sweep > 0)
                 def _():
-                    take_state(sweep, fresh - 2)
-
-            if fresh == 1:
+                    for row in late:
+                        take_state(sweep, row)
+
+            if 1 in fresh:
                 wait_halo(sweep)
-            value = first[index] + conv(w_one, cols_one, index)
-            if fresh is not None:
-                build(sweep, fresh)
+            value = conv_pair(w_one, cols_one, pair)
+            for index in fresh:
+                build(sweep, index)
+            slot = 2 * (turn % 2)
             if before is not None:
-                activate_one(before)
-            first[index] = value
-            sums_one[index % 2] = value
-            before = index
+                for half, index in enumerate(before):
+                    activate_one(index, 2 - slot + half)
+            for half, index in enumerate(pair):
+                part = first[index] + value[:, half * width : (half + 1) * width]
+                first[index] = part
+                sums_one[slot + half] = part
+            before, last = pair, slot
 
         @pl.when(sweep == 0)
         def _():
             loads[5].wait()
             build_weight(raw_two, w_two)
 
+        pairs = [edges[:2], edges[2:]]
+        pairs += [middle[place : place + 2] for place in range(0, len(middle), 2)]
+        for half, index in enumerate(before):
+            activate_one(index, last + half)
         done = None
-        for row in edges + tuple(range(2, height - 2)):
-            value = first[row + 1] + conv(w_two, cols_two, row)
-            if done is None:
-                activate_one(before)
-            else:
-                finish_row(sweep, done)
-            sums_two[row % 2] = value
+        for turn, pair in enumerate(pairs):
+            value = conv_pair(w_two, cols_two, pair)
+            slot = 2 * (turn % 2)
             if done is not None:
-                send_drift(sweep, done)
-            done = row
-        finish_row(sweep, done)
-        send_drift(sweep, done)
+                finish_pair(sweep, done, 2 - slot)
+            for half, row in enumerate(pair):
+                sums_two[slot + half] = (
+                    first[row + 1] + value[:, half * width : (half + 1) * width]
+                )
+            if done is not None:
+                for row in done:
+                    send_drift(sweep, row)
+            done = pair
+        finish_pair(sweep, done, slot)
+        for row in done:
+            send_drift(sweep, row)
 
     loads[0].wait()
     for row in range(height):
@@ -372,9 +394,9 @@
                 pltpu.VMEM(((height + 4) * block, width), jnp.bfloat16),
                 pltpu.VMEM(((height + 2) * block, width), jnp.bfloat16),
                 pltpu.VMEM((height + 2, feats, width), jnp.float32),
-                pltpu.VMEM((2, feats, width), jnp.float32),
-                pltpu.VMEM((2, feats, width), jnp.float32),
-                pltpu.VMEM((2, feats, width), jnp.bfloat16),
+                pltpu.VMEM((4, feats, width), jnp.float32),
+                pltpu.VMEM((4, feats, width), jnp.float32),
+                pltpu.VMEM((2, feats, 2 * width), jnp.bfloat16),
                 pltpu.VMEM((height, chans, width), jnp.float32),
                 pltpu.VMEM((height, chans, width), jnp.float32),
                 pltpu.VMEM((ITERS, height + 4, chans, width), jnp.bfloat16),

time: 45.6 us -> 37.5 us (0.82)
  Pallas kernels: 42.5 us -> 34.4 us
    pallas_call x1, Pallas kernels: 42.5 us -> 34.4 us  [per_device(): pl.pallas_call(functools.partial(kernel, steps, tiles), out_shape=jax.Sha...]
where the time goes in v3:
time: 37.5 us; the launch traced here: 37.3 us
  Pallas kernels  34.4 us (92%)
  local copies, waits for them, and re-layouts  1.57 us (4%)
  between operations  1.3 us (3%)
    pallas_call x1, Pallas kernels, per_device(): pl.pallas_call(functools.partial(kernel, steps, tiles), out_shape=jax.Sha...  34.4 us
    unnamed x1, local copies, waits for them, and re-layouts  1.57 us

profile of v3, /device:TPU:0, one launch (start us, length us, event | category | flops | bytes accessed | tf_op | source)
XLA Modules:
  0.0 37.3 jit_solution(6337334081204163521)
XLA Ops:
  1.3 34.4 %shard_map.82 = f32[1,16,8,256]{3,2,1,0:T(8,128)} custom-call(f32[16,8,256]{2,1,0:T(8,128)} %x_hbm.1, f32[1,320]{1,0:T(1,128)} %embed_hbm.1, f32[1]{0:T(128)S(6)} %copy.10.scale_ref, f32[1]{0:T(128)S(6)} %copy.11.decay_ref, bf16[16,320]{1,0:T(8,128)(2,1)} %bitcast.1, bf16[16,320]{1,0:T(8,128)(2,1)} %project_hbm.1, bf16[3,3,320,320]{3,2,1,0:T(8,128)(2,1)} %conv_one_hbm.1, ...), custom_call_target="tpu_custom_call" | custom-call | tf_op jit(solution)/shard_map/pallas_call | solution.py:378
  35.7 1.6 %copy.12 = f32[1,16,8,256]{3,2,1,0:T(8,128)} copy(f32[1,16,8,256]{3,2,1,0:T(8,128)} %shard_map.82) | data formatting | bytes 262144

commit v4 on v3

--- a/solution.py
+++ b/solution.py
@@ -171,23 +171,21 @@
         cols[base + feats : base + feats + chunk, :] = mid
         cols[base + 2 * feats : base + 2 * feats + chunk, :] = right
 
-    def build(sweep, index):
+    def lift(sweep, pair):
+        xb = jnp.concatenate([xb_rows[sweep, index] for index in pair], axis=1)
+        value = jnp.dot(lift_rows[:, :chans], xb, preferred_element_type=jnp.float32)
+        embed = jnp.concatenate([embed_bc[...]] * (width // 128), axis=1)
+        for half, index in enumerate(pair):
+            first[index] = value[:, half * width : (half + 1) * width] + embed
+
+    def build(index):
         inside = None
         if index < 2:
             inside = has_up
         if index >= height + 2:
             inside = has_down
-        xb = xb_rows[sweep, index]
         for start in range(0, feats, chunk):
-            lifted = jnp.dot(
-                lift_rows[start : start + chunk, :chans], xb, preferred_element_type=jnp.float32
-            )
-            lifted = lifted + jnp.concatenate(
-                [embed_bc[start : start + chunk, :]] * (width // 128), axis=1
-            )
-            if 1 <= index <= height + 2:
-                first[index - 1, start : start + chunk, :] = lifted
-            act = silu(lifted)
+            act = silu(first[index, start : start + chunk, :])
             if inside is not None:
                 act = jnp.where(inside, act, 0.0)
             store_columns(cols_one, index, start, act)
@@ -222,8 +220,8 @@
             part = out[:, half * width : (half + 1) * width]
             drift_out[sweep, row] = scale_ref[0] * part - decay_ref[0] * state_rows[row]
 
-    def build_weight(raw, weight):
-        for tap in range(9):
+    def build_weight(raw, weight, taps=range(9)):
+        for tap in taps:
             weight[:, tap * feats : (tap + 1) * feats] = raw[tap // 3, tap % 3]
 
     def take_state(sweep, row):
@@ -237,14 +235,13 @@
 
         @pl.when(sweep > 0)
         def _():
-            for row in edges:
+            for row in range(4):
                 take_state(sweep, row)
-            send_halo(sweep)
-            take_state(sweep, 2)
-            take_state(sweep, 3)
-
+
+        for pair in ((2, 3), (4, 5)):
+            lift(sweep, pair)
         for index in (2, 3, 4, 5):
-            build(sweep, index)
+            build(index)
 
         @pl.when(sweep == 0)
         def _():
@@ -258,47 +255,55 @@
         before = None
         for turn, pair in enumerate(order):
             fresh = builds[turn]
-            late = [index - 2 for index in fresh if 6 <= index < height]
-            if late:
+            if turn == 0:
 
                 @pl.when(sweep > 0)
                 def _():
-                    for row in late:
+                    for row in range(height - 1, 3, -1):
                         take_state(sweep, row)
+                    send_halo(sweep)
 
             if 1 in fresh:
                 wait_halo(sweep)
+            if fresh:
+                lift(sweep, fresh)
+            if turn == len(order) - 2:
+
+                @pl.when(sweep == 0)
+                def _():
+                    loads[5].wait()
+
             value = conv_pair(w_one, cols_one, pair)
+            if turn == len(order) - 2:
+                build_weight(raw_two, w_two, range(2))
+            if turn == len(order) - 1:
+                build_weight(raw_two, w_two, range(2, 9))
             for index in fresh:
-                build(sweep, index)
+                build(index)
             slot = 2 * (turn % 2)
             if before is not None:
                 for half, index in enumerate(before):
                     activate_one(index, 2 - slot + half)
             for half, index in enumerate(pair):
-                part = first[index] + value[:, half * width : (half + 1) * width]
-                first[index] = part
+                part = first[index + 1] + value[:, half * width : (half + 1) * width]
+                first[index + 1] = part
                 sums_one[slot + half] = part
             before, last = pair, slot
 
-        @pl.when(sweep == 0)
-        def _():
-            loads[5].wait()
-            build_weight(raw_two, w_two)
-
-        pairs = [edges[:2], edges[2:]]
-        pairs += [middle[place : place + 2] for place in range(0, len(middle), 2)]
-        for half, index in enumerate(before):
-            activate_one(index, last + half)
+        pairs = [middle[:2], edges[:2], edges[2:]]
+        pairs += [middle[place : place + 2] for place in range(2, len(middle), 2)]
         done = None
         for turn, pair in enumerate(pairs):
             value = conv_pair(w_two, cols_two, pair)
             slot = 2 * (turn % 2)
-            if done is not None:
+            if done is None:
+                for half, index in enumerate(before):
+                    activate_one(index, last + half)
+            else:
                 finish_pair(sweep, done, 2 - slot)
             for half, row in enumerate(pair):
                 sums_two[slot + half] = (
-                    first[row + 1] + value[:, half * width : (half + 1) * width]
+                    first[row + 2] + value[:, half * width : (half + 1) * width]
                 )
             if done is not None:
                 for row in done:
@@ -374,7 +379,7 @@
         peers = max(steps - 1, 1)
         vmem = pl.BlockSpec(memory_space=pltpu.VMEM)
         smem = pl.BlockSpec(memory_space=pltpu.SMEM)
-        hbm = pl.BlockSpec(memory_space=pl.ANY)
+        hbm = pl.BlockSpec(memory_space=pltpu.HBM)
         return pl.pallas_call(
             functools.partial(kernel, steps, tiles),
             out_shape=jax.ShapeDtypeStruct((1, chans, height, width), jnp.float32),
@@ -393,7 +398,7 @@
                 pltpu.VMEM((feats, 128), jnp.bfloat16),
                 pltpu.VMEM(((height + 4) * block, width), jnp.bfloat16),
                 pltpu.VMEM(((height + 2) * block, width), jnp.bfloat16),
-                pltpu.VMEM((height + 2, feats, width), jnp.float32),
+                pltpu.VMEM((height + 4, feats, width), jnp.float32),
                 pltpu.VMEM((4, feats, width), jnp.float32),
                 pltpu.VMEM((4, feats, width), jnp.float32),
                 pltpu.VMEM((2, feats, 2 * width), jnp.bfloat16),

time: 37.5 us -> 35.9 us (0.957)
  Pallas kernels: 34.4 us -> 32.6 us
    pallas_call x1, Pallas kernels: 34.4 us -> 32.6 us  [per_device(): pl.pallas_call(functools.partial(kernel, steps, tiles), out_shape=jax.Sha...]
where the time goes in v4:
time: 35.9 us; the launch traced here: 35.5 us
  Pallas kernels  32.6 us (91%)
  local copies, waits for them, and re-layouts  1.57 us (4%)
  between operations  1.3 us (4%)
    pallas_call x1, Pallas kernels, per_device(): pl.pallas_call(functools.partial(kernel, steps, tiles), out_shape=jax.Sha...  32.6 us
    unnamed x1, local copies, waits for them, and re-layouts  1.57 us

profile of v4, /device:TPU:0, one launch (start us, length us, event | category | flops | bytes accessed | tf_op | source)
XLA Modules:
  0.0 35.5 jit_solution(16048590917028137723)
XLA Ops:
  1.3 32.6 %shard_map.82 = f32[1,16,8,256]{3,2,1,0:T(8,128)} custom-call(f32[16,8,256]{2,1,0:T(8,128)} %x_hbm.1, f32[1,320]{1,0:T(1,128)} %embed_hbm.1, f32[1]{0:T(128)S(6)} %copy.10.scale_ref, f32[1]{0:T(128)S(6)} %copy.11.decay_ref, bf16[16,320]{1,0:T(8,128)(2,1)} %bitcast.1, bf16[16,320]{1,0:T(8,128)(2,1)} %project_hbm.1, bf16[3,3,320,320]{3,2,1,0:T(8,128)(2,1)} %conv_one_hbm.1, ...), custom_call_target="tpu_custom_call" | custom-call | tf_op jit(solution)/shard_map/pallas_call | solution.py:383
  33.9 1.6 %copy.12 = f32[1,16,8,256]{3,2,1,0:T(8,128)} copy(f32[1,16,8,256]{3,2,1,0:T(8,128)} %shard_map.82) | data formatting | bytes 262144

commit v5 on v4

--- a/solution.py
+++ b/solution.py
@@ -131,31 +131,33 @@
         def _():
             up.wait_recv()
 
-    def drift_copy(sweep, shift, row):
+    def drift_copy(sweep, shift, pair):
         return pltpu.make_async_remote_copy(
-            src_ref=drift_out.at[sweep, row],
-            dst_ref=drift_in.at[sweep, shift - 1, row],
-            send_sem=drift_send.at[sweep, shift - 1, row],
-            recv_sem=drift_recv.at[sweep, shift - 1, row],
+            src_ref=drift_out.at[sweep, pl.ds(2 * pair, 2)],
+            dst_ref=drift_in.at[sweep, shift - 1, pl.ds(2 * pair, 2)],
+            send_sem=drift_send.at[sweep, shift - 1, pair],
+            recv_sem=drift_recv.at[sweep, shift - 1, pair],
             device_id=(tm + shift, space),
             device_id_type=MESH,
         )
 
-    def send_drift(sweep, row):
+    def send_drift(sweep, pair):
         for shift in range(1, steps):
 
             @pl.when(tm + shift < steps)
             def _():
-                drift_copy(sweep, shift, row).start()
+                drift_copy(sweep, shift, pair).start()
+
+    def wait_drift(sweep, pair):
+        for shift in range(1, steps):
+
+            @pl.when(tm >= shift)
+            def _():
+                drift_copy(sweep, shift, pair).wait_recv()
 
     def earlier(sweep, row):
         total = jnp.zeros((chans, width), jnp.float32)
         for shift in range(1, steps):
-
-            @pl.when(tm >= shift)
-            def _():
-                drift_copy(sweep, shift, row).wait_recv()
-
             total = total + jnp.where(tm >= shift, drift_in[sweep, shift - 1, row], 0.0)
         return total
 
@@ -224,19 +226,21 @@
         for tap in taps:
             weight[:, tap * feats : (tap + 1) * feats] = raw[tap // 3, tap % 3]
 
-    def take_state(sweep, row):
-        state = rows_f32[row] + earlier(sweep - 1, row)
-        state_rows[row] = state
-        xb_rows[sweep, row + 2] = state.astype(jnp.bfloat16)
+    def take_states(sweep, pair):
+        wait_drift(sweep - 1, pair)
+        for row in (2 * pair, 2 * pair + 1):
+            state = rows_f32[row] + earlier(sweep - 1, row)
+            state_rows[row] = state
+            xb_rows[sweep, row + 2] = state.astype(jnp.bfloat16)
 
     def one_sweep(sweep):
-        edges = (0, 1, height - 1, height - 2)
+        edges = (0, 1, height - 2, height - 1)
         middle = tuple(range(2, height - 2))
 
         @pl.when(sweep > 0)
         def _():
-            for row in range(4):
-                take_state(sweep, row)
+            for pair in range(2):
+                take_states(sweep, pair)
 
         for pair in ((2, 3), (4, 5)):
             lift(sweep, pair)
@@ -259,8 +263,8 @@
 
                 @pl.when(sweep > 0)
                 def _():
-                    for row in range(height - 1, 3, -1):
-                        take_state(sweep, row)
+                    for rest in range(height // 2 - 1, 1, -1):
+                        take_states(sweep, rest)
                     send_halo(sweep)
 
             if 1 in fresh:
@@ -306,12 +310,10 @@
                     first[row + 2] + value[:, half * width : (half + 1) * width]
                 )
             if done is not None:
-                for row in done:
-                    send_drift(sweep, row)
+                send_drift(sweep, done[0] // 2)
             done = pair
         finish_pair(sweep, done, slot)
-        for row in done:
-            send_drift(sweep, row)
+        send_drift(sweep, done[0] // 2)
 
     loads[0].wait()
     for row in range(height):
@@ -337,6 +339,8 @@
     def _(sweep):
         one_sweep(sweep)
 
+    for pair in range(height // 2):
+        wait_drift(ITERS - 1, pair)
     for row in range(height):
         total = drift_out[ITERS - 1, row] + earlier(ITERS - 1, row)
         out_ref[0, :, row, :] = rows_f32[row] + total
@@ -353,11 +357,11 @@
             down.wait_send()
 
         for shift in range(1, steps):
-            for row in range(height):
+            for pair in range(height // 2):
 
                 @pl.when(tm + shift < steps)
                 def _():
-                    drift_copy(sweep, shift, row).wait_send()
+                    drift_copy(sweep, shift, pair).wait_send()
 
 
 def solution(mesh):
@@ -410,8 +414,8 @@
                 pltpu.SemaphoreType.DMA((6,)),
                 pltpu.SemaphoreType.DMA((ITERS, 2)),
                 pltpu.SemaphoreType.DMA((ITERS, 2)),
-                pltpu.SemaphoreType.DMA((ITERS, peers, height)),
-                pltpu.SemaphoreType.DMA((ITERS, peers, height)),
+                pltpu.SemaphoreType.DMA((ITERS, peers, height // 2)),
+                pltpu.SemaphoreType.DMA((ITERS, peers, height // 2)),
             ],
             compiler_params=pltpu.CompilerParams(
                 collective_id=0, has_side_effects=True, vmem_limit_bytes=67043328

time: 35.9 us -> 35.2 us (0.981)
  Pallas kernels: 32.6 us -> 32.1 us
    pallas_call x1, Pallas kernels: 32.6 us -> 32.1 us  [per_device(): pl.pallas_call(functools.partial(kernel, steps, tiles), out_shape=jax.Sha...]
where the time goes in v5:
time: 35.2 us; the launch traced here: 35 us
  Pallas kernels  32.1 us (91%)
  local copies, waits for them, and re-layouts  1.57 us (4%)
  between operations  1.3 us (4%)
    pallas_call x1, Pallas kernels, per_device(): pl.pallas_call(functools.partial(kernel, steps, tiles), out_shape=jax.Sha...  32.1 us
    unnamed x1, local copies, waits for them, and re-layouts  1.57 us

profile of v5, /device:TPU:0, one launch (start us, length us, event | category | flops | bytes accessed | tf_op | source)
XLA Modules:
  0.0 35.0 jit_solution(17783385885195890966)
XLA Ops:
  1.3 32.1 %shard_map.82 = f32[1,16,8,256]{3,2,1,0:T(8,128)} custom-call(f32[16,8,256]{2,1,0:T(8,128)} %x_hbm.1, f32[1,320]{1,0:T(1,128)} %embed_hbm.1, f32[1]{0:T(128)S(6)} %copy.10.scale_ref, f32[1]{0:T(128)S(6)} %copy.11.decay_ref, bf16[16,320]{1,0:T(8,128)(2,1)} %bitcast.1, bf16[16,320]{1,0:T(8,128)(2,1)} %project_hbm.1, bf16[3,3,320,320]{3,2,1,0:T(8,128)(2,1)} %conv_one_hbm.1, ...), custom_call_target="tpu_custom_call" | custom-call | tf_op jit(solution)/shard_map/pallas_call | solution.py:387
  33.4 1.6 %copy.12 = f32[1,16,8,256]{3,2,1,0:T(8,128)} copy(f32[1,16,8,256]{3,2,1,0:T(8,128)} %shard_map.82) | data formatting | bytes 262144
